TPU v7x, 32 devices: a whole 2x2x4 slice. The times are simulated.
32 devices in a mesh: space: 16 (over z, y, core), filt: 2 (over x).
Axes of the slice: x: 2, y: 2, z: 4, core: 2. Of those that a mesh axis runs over, the one named last changes fastest.
Arguments:
- volume: bfloat16 [64, 32, 4, 256], P(None, 'space', 'filt'), may hold values from -6 to 6
- first_weight: bfloat16 [27, 64, 64], replicated, may hold values from -0.15625 to 0.15625
- second_weight: bfloat16 [27, 128, 64], P(None, 'filt'), may hold values from -0.15625 to 0.15625
- cotangent: bfloat16 [128, 16, 2, 128], P('filt', 'space'), may hold values from -24 to 24
Outputs:
- features: bfloat16 [128, 16, 2, 128], P('filt', 'space')
- volume_grad: bfloat16 [64, 32, 4, 256], P(None, 'space', 'filt')
- first_grad: float32 [27, 64, 64], replicated
- second_grad: float32 [27, 128, 64], P(None, 'filt')
All inputs are finite; a program needn't handle non-finite values.
Results may differ from a plain program's by a relative error of at most 0.019.
Values may be sent and summed in bfloat16 or wider, within the bound.
No kernel may reach another device: no remote copies, remote signals or barrier semaphores. Data moves between devices by JAX's collectives and lax.ppermute only.
A program may use at most 64 MiB of HBM per device.

v0:
```python
import jax
import jax.numpy as jnp
from jax import lax
from jax.sharding import PartitionSpec as P


def extended(cells, sides, width):
    for axis, dim in sides:
        count = lax.axis_size(axis)
        ends = count - 1
        head = lax.slice_in_dim(cells, 0, width, axis=dim)
        tail = lax.slice_in_dim(cells, cells.shape[dim] - width, cells.shape[dim], axis=dim)
        cells = jnp.concatenate(
            [
                lax.ppermute(tail, axis, [(i, (i + 1) % count) for i in range(ends)]),
                cells,
                lax.ppermute(head, axis, [((i + 1) % count, i) for i in range(ends)]),
            ],
            axis=dim,
        )
    return cells


def silu_slope(values):
    sigmoid_part = jax.nn.sigmoid(values)
    return sigmoid_part * (1.0 + values * (1.0 - sigmoid_part))


def pad_depth(volume_field):
    return jnp.pad(volume_field, ((0, 0), (0, 0), (0, 0), (1, 1)))


def window(padded, offset_x, offset_y, offset_z, extents):
    extent_x, extent_y, extent_z = extents
    section = lax.slice(
        padded,
        (0, offset_x, offset_y, offset_z),
        (padded.shape[0], offset_x + extent_x, offset_y + extent_y, offset_z + extent_z),
    )
    return section.reshape(padded.shape[0], extent_x * extent_y * extent_z)


def conv_forward(padded, weight, extents):
    outputs, inputs = (weight.shape[1], weight.shape[2])
    running = jnp.zeros((outputs, extents[0] * extents[1] * extents[2]), jnp.float32)
    for offset_x in range(3):
        for offset_y in range(3):
            tap_base = offset_x * 9 + offset_y * 3
            stacked = jnp.concatenate(
                [window(padded, offset_x, offset_y, offset_z, extents) for offset_z in range(3)],
                axis=0,
            )
            matrices = jnp.transpose(weight[tap_base : tap_base + 3], (1, 0, 2)).reshape(
                outputs, 3 * inputs
            )
            running = running + jnp.dot(matrices, stacked, preferred_element_type=jnp.float32)
    return running


def conv_transpose(padded, weight, extents):
    outputs, inputs = (weight.shape[1], weight.shape[2])
    running = jnp.zeros((inputs, extents[0] * extents[1] * extents[2]), jnp.float32)
    for offset_x in range(3):
        for offset_y in range(3):
            tap_base = offset_x * 9 + offset_y * 3
            stacked = jnp.concatenate(
                [window(padded, offset_x, offset_y, offset_z, extents) for offset_z in range(3)],
                axis=0,
            )
            tap_block = weight[24 - tap_base : 27 - tap_base][::-1]
            matrices = jnp.transpose(tap_block, (2, 0, 1)).reshape(inputs, 3 * outputs)
            running = running + jnp.dot(matrices, stacked, preferred_element_type=jnp.float32)
    return running


def conv_weights(grad_rows, padded, extents):
    outputs, inputs = (grad_rows.shape[0], padded.shape[0])
    blocks = []
    for offset_x in range(3):
        for offset_y in range(3):
            stacked = jnp.concatenate(
                [window(padded, offset_x, offset_y, offset_z, extents) for offset_z in range(3)],
                axis=0,
            )
            section = lax.dot_general(
                grad_rows, stacked, (((1,), (1,)), ((), ())), preferred_element_type=jnp.float32
            )
            blocks.append(jnp.transpose(section.reshape(outputs, 3, inputs), (1, 0, 2)))
    return jnp.concatenate(blocks, axis=0)


def pool_cells(hidden):
    channels, size_x, size_y, size_z = hidden.shape
    pair_table = (jnp.arange(size_z)[:, None] // 2 == jnp.arange(size_z // 2)[None, :]).astype(
        jnp.bfloat16
    )
    depth_sums = jnp.dot(hidden.reshape(-1, size_z), pair_table, preferred_element_type=jnp.float32)
    depth_sums = depth_sums.reshape(channels, size_x // 2, 2, size_y // 2, 2, size_z // 2)
    return (0.125 * depth_sums.sum(axis=(2, 4))).astype(jnp.bfloat16)


def spread_cells(grad_field):
    scaled = 0.125 * grad_field
    scaled = jnp.repeat(scaled, 2, axis=1)
    scaled = jnp.repeat(scaled, 2, axis=2)
    return jnp.repeat(scaled, 2, axis=3)


def local(volume, first_weight, second_weight, cotangent):
    count_space = lax.axis_size("space")
    count_filt = lax.axis_size("filt")
    channels = volume.shape[0]
    fine_shape = volume.shape[1:]
    fine_cells = fine_shape[0] * fine_shape[1] * fine_shape[2] * count_space * count_filt
    fine_scale = 1.0 / fine_cells**0.5
    padded_in = pad_depth(extended(volume, (("space", 1), ("filt", 2)), 1))
    first_pre = conv_forward(padded_in, first_weight, fine_shape)
    hidden = jax.nn.silu(first_pre).astype(jnp.bfloat16).reshape((channels,) + fine_shape)
    pooled = pool_cells(hidden)
    brick_shape = pooled.shape[1:]
    brick_cells = brick_shape[0] * brick_shape[1] * brick_shape[2]
    bottom_scale = 1.0 / (brick_cells * count_space * count_filt) ** 0.5
    filters = second_weight.shape[1]
    whole_weight = lax.all_gather(second_weight, "filt", axis=1, tiled=True)
    total_filters = whole_weight.shape[1]
    padded_pool = pad_depth(extended(pooled, (("space", 1), ("filt", 2)), 1))
    second_pre = conv_forward(padded_pool, whole_weight, brick_shape)
    local_out = jax.nn.silu(second_pre).astype(jnp.bfloat16).reshape((total_filters,) + brick_shape)
    features = lax.all_to_all(local_out, "filt", split_axis=0, concat_axis=2, tiled=True)
    local_cot = lax.all_to_all(cotangent, "filt", split_axis=2, concat_axis=0, tiled=True)
    down_grad = (
        local_cot.reshape(total_filters, -1).astype(jnp.float32) * silu_slope(second_pre)
    ).astype(jnp.bfloat16)
    summed = lax.psum(conv_weights(down_grad, padded_pool, brick_shape), ("space", "filt"))
    second_grad = (
        lax.dynamic_slice_in_dim(summed, lax.axis_index("filt") * filters, filters, 1)
        * bottom_scale
    )
    padded_down = pad_depth(
        extended(down_grad.reshape((total_filters,) + brick_shape), (("space", 1), ("filt", 2)), 1)
    )

    def add_group(group_index, running):
        group_rows = lax.dynamic_slice_in_dim(padded_down, group_index * filters, filters, 0)
        tap_block = lax.dynamic_slice_in_dim(whole_weight, group_index * filters, filters, 1)
        section = conv_transpose(group_rows, tap_block, brick_shape)
        return running + lax.optimization_barrier(section.astype(jnp.bfloat16)).astype(jnp.float32)

    pool_grad = lax.fori_loop(
        0, count_filt, add_group, jnp.zeros((channels, brick_cells), jnp.float32)
    )
    hidden_grad = spread_cells(pool_grad.reshape((channels,) + brick_shape))
    first_down = (hidden_grad.reshape(channels, -1) * silu_slope(first_pre)).astype(jnp.bfloat16)
    first_grad = (
        lax.psum(conv_weights(first_down, padded_in, fine_shape), ("space", "filt")) * fine_scale
    )
    padded_back = pad_depth(
        extended(first_down.reshape((channels,) + fine_shape), (("space", 1), ("filt", 2)), 1)
    )
    volume_grad = (
        conv_transpose(padded_back, first_weight, fine_shape)
        .astype(jnp.bfloat16)
        .reshape((channels,) + fine_shape)
    )
    return (features, volume_grad, first_grad, second_grad)


def solution(mesh):
    placed = (
        P(None, "space", "filt", None),
        P(),
        P(None, "filt", None),
        P("filt", "space", None, None),
    )
    return jax.shard_map(
        local,
        mesh=mesh,
        in_specs=placed,
        out_specs=(
            P("filt", "space", None, None),
            P(None, "space", "filt", None),
            P(),
            P(None, "filt", None),
        ),
        check_vma=False,
    )
```

profile of v0, /device:TPU:0, one launch (start us, length us, event | category | flops | bytes accessed | tf_op | source)
XLA Modules:
  0.0 316.7 jit_solution(11860188222224926915)
XLA Ops:
  7.2 1.4 copy.107
  8.5 4.2 %all-to-all-start.1 = ((bf16[64,1,2,128]{3,0,1,2:T(8,128)(2,1)}), bf16[64,1,2,128]{3,0,1,2:T(8,128)(2,1)}, u32[]{:S(2)}, u32[]{:S(2)}) async-start(bf16[64,1,2,128]{3,0,1,2:T(8,128)(2,1)} %copy.107), calls=%async_computation.1 | async-start | bytes 65536 | tf_op jit(solution)/shard_map/all_to_all | solution.py:130
  12.8 1.0 fusion.162
  13.7 1.3 collective-permute-start.1
  15.0 3.0 collective-permute-start
  18.1 1.3 copy.96
  19.4 15.2 %all_gather.3 = bf16[27,128,64]{2,0,1:T(8,128)(2,1)S(1)} all-gather(bf16[27,64,64]{2,0,1:T(8,128)(2,1)S(1)} %copy.96), channel_id=1, replica_groups=mesh['space'=16,'filt'=2] {'filt'}, dimensions={1}, use_global_device_ids=true | all-gather | bytes 663552 | tf_op jit(solution)/shard_map/all_gather | solution.py:124
  34.6 1.3 fusion.155
  36.4 1.2 fusion.160
  37.6 4.2 %collective-permute-start.2 = (bf16[64,4,1,256]{3,2,1,0:T(2,128)(2,1)}, bf16[64,4,1,256]{3,2,1,0:T(2,128)(2,1)S(1)}, u32[]{:S(2)}, u32[]{:S(2)}) collective-permute-start(bf16[64,4,1,256]{3,2,1,0:T(2,128)(2,1)} %get-tuple-element.266), channel_id=1, source_target_pairs={{0,1},{2,3},{4,5},{6,7},{8,9},{10,11},{12,13},{14,15},{16,17},{18,... | collective-permute-start | bytes 393224 | tf_op jit(solution)/shard_map/ppermute | solution.py:15
  41.8 1.5 collective-permute-start.3
  43.3 1.0 fusion.158
  45.5 1.8 copy.153
  47.3 1.0 copy.152
  48.3 1.6 copy.151
  50.0 1.6 copy.150
  51.6 1.6 copy.149
  56.1 1.4 rev.98
  70.2 1.7 pad_maximum_fusion.9
  75.6 2.4 select_maximum_fusion.2
  78.1 2.9 fusion.157
  86.4 1.0 constant_dynamic-update-slice_fusion.11
  93.1 1.3 collective-permute-start.5
  94.4 3.0 collective-permute-start.4
  98.4 1.3 collective-permute-start.7
  99.7 4.8 %collective-permute-start.6 = (bf16[64,3,1,128]{3,0,2,1:T(8,128)(2,1)S(1)}, bf16[64,3,1,128]{3,0,2,1:T(8,128)(2,1)S(1)}, u32[]{:S(2)}, u32[]{:S(2)}) collective-permute-start(bf16[64,3,1,128]{3,0,2,1:T(8,128)(2,1)S(1)} %pad_maximum_fusion.18), channel_id=1, source_target_pairs={{0,1},{2,3},{4,5},{6,7},{8,9},{10,11},{12,13},{14,15},{16,17},{18,... | collective-permute-start | bytes 147464 | tf_op jit(solution)/shard_map/ppermute | solution.py:15
  104.5 1.5 collective-permute-done.6
  108.2 1.3 collective-permute-start.9
  109.5 3.3 %collective-permute-start.8 = (bf16[128,1,1,128]{0,3,2,1:T(8,128)(2,1)S(1)}, bf16[128,1,1,128]{0,3,2,1:T(8,128)(2,1)S(1)}, u32[]{:S(2)}, u32[]{:S(2)}) collective-permute-start(bf16[128,1,1,128]{0,3,2,1:T(8,128)(2,1)S(1)} %bitcast.409), channel_id=1, source_target_pairs={{0,2},{2,4},{4,6},{6,8},{8,10},{10,12},{12,14},{14,16},{16,18},{18... | collective-permute-start | bytes 98312 | tf_op jit(solution)/shard_map/ppermute | solution.py:15
  115.9 3.3 %all-to-all-start = ((bf16[2,2,4096]{2,1,0:T(2,128)(2,1)}), bf16[2,2,4096]{2,1,0:T(2,128)(2,1)S(1)}, u32[]{:S(2)}, u32[]{:S(2)}) async-start(bf16[2,2,4096]{2,1,0:T(2,128)(2,1)} %reshape.942), calls=%async_computation | async-start | bytes 65536 | tf_op jit(solution)/shard_map/all_to_all | solution.py:129
  128.8 1.3 collective-permute-start.11
  130.1 4.6 %collective-permute-start.10 = (bf16[128,3,1,128]{0,3,2,1:T(8,128)(2,1)S(1)}, bf16[128,3,1,128]{0,3,2,1:T(8,128)(2,1)S(1)}, u32[]{:S(2)}, u32[]{:S(2)}) collective-permute-start(bf16[128,3,1,128]{0,3,2,1:T(8,128)(2,1)S(1)} %pad_maximum_fusion.17), channel_id=1, source_target_pairs={{0,1},{2,3},{4,5},{6,7},{8,9},{10,11},{12,13},{14,15},{16,17},{18,... | collective-permute-start | bytes 294920 | tf_op jit(solution)/shard_map/ppermute | solution.py:15
  135.6 1.3 collective-permute-done.10
  137.4 5.5 %while.14 = (s32[]{:T(128)}, f32[64,128]{1,0:T(8,128)}, bf16[27,128,64]{2,1,0:T(8,128)(2,1)S(1)}, bf16[128,3,3,130]{3,0,2,1:T(8,128)(2,1)S(1)}, s32[]{:T(128)}, ...) while((s32[]{:T(128)}, f32[64,128]{1,0:T(8,128)}, ...), condition=%wide.region_2.3_spmd.clone, body=%wide.region_1.2_spmd.clone.sunk | while | flops 29736976 | bytes 3318213 | solution.py:149
  147.0 1.3 collective-permute-start.13
  148.3 4.5 %collective-permute-start.12 = (bf16[64,1,2,256]{3,2,1,0:T(2,128)(2,1)S(1)}, bf16[64,1,2,256]{3,2,1,0:T(2,128)(2,1)S(1)}, u32[]{:S(2)}, u32[]{:S(2)}) collective-permute-start(bf16[64,1,2,256]{3,2,1,0:T(2,128)(2,1)S(1)} %get-tuple-element.272), channel_id=1, source_target_pairs={{0,2},{2,4},{4,6},{6,8},{8,10},{10,12},{12,14},{14,16},{16,18},{18... | collective-permute-start | bytes 196616 | tf_op jit(solution)/shard_map/ppermute | solution.py:15
  154.6 4.0 %collective-permute-start.14 = (bf16[64,4,1,256]{3,2,1,0:T(2,128)(2,1)S(1)}, bf16[64,4,1,256]{3,2,1,0:T(2,128)(2,1)S(1)}, u32[]{:S(2)}, u32[]{:S(2)}) collective-permute-start(bf16[64,4,1,256]{3,2,1,0:T(2,128)(2,1)S(1)} %get-tuple-element.261), channel_id=1, source_target_pairs={{0,1},{2,3},{4,5},{6,7},{8,9},{10,11},{12,13},{14,15},{16,17},{18,... | collective-permute-start | bytes 393224 | tf_op jit(solution)/shard_map/ppermute | solution.py:15
  158.6 1.6 collective-permute-start.15
  161.3 2.3 collective-permute-done.14
  163.6 4.7 %collective-permute-done.15 = bf16[64,4,1,256]{3,2,1,0:T(2,128)(2,1)S(1)} collective-permute-done((bf16[64,4,1,256]{3,2,1,0:T(2,128)(2,1)S(1)}, bf16[64,4,1,256]{3,2,1,0:T(2,128)(2,1)S(1)}, u32[]{:S(2)}, u32[]{:S(2)}) %collective-permute-start.15) | collective-permute-done | bytes 131104 | tf_op jit(solution)/shard_map/ppermute | solution.py:17
  168.3 1.7 pad_maximum_fusion.1
  172.4 2.4 select_maximum_fusion
  174.8 2.9 fusion.156
  181.8 1.2 fusion.62
  186.0 120.2 %all-reduce.7.cloned.1.call-done = (f32[27,64,64]{1,2,0:T(8,128)}, f32[27,128,64]{2,1,0:T(8,128)}) async-done(((f32[27,64,64]{1,2,0:T(8,128)}, f32[27,128,64]{2,1,0:T(8,128)}), (f32[27,64,64]{1,2,0:T(8,128)}, f32[27,128,64]{2,1,0:T(8,128)})) %all-reduce.7.cloned.1.call-update) | async-done | bytes 1327120 | tf_op jit(solution)/shard_map/psum | solution.py:155
  306.2 1.4 broadcast_multiply_fusion
  307.6 1.2 copy.133
  308.9 1.0 dynamic-slice_multiply_fusion
  (459 shorter events, 69.2 us)
Async XLA Ops:
  8.5 88.9 %all-to-all-start.1 = ((bf16[64,1,2,128]{3,0,1,2:T(8,128)(2,1)}), bf16[64,1,2,128]{3,0,1,2:T(8,128)(2,1)}, u32[]{:S(2)}, u32[]{:S(2)}) async-start(bf16[64,1,2,128]{3,0,1,2:T(8,128)(2,1)} %copy.107), calls=%async_computation.1 | async-start | bytes 65536 | tf_op jit(solution)/shard_map/all_to_all | solution.py:130
  13.7 22.2 %collective-permute-start.1 = (bf16[64,1,2,256]{3,2,1,0:T(2,128)(2,1)S(1)}, bf16[64,1,2,256]{3,2,1,0:T(2,128)(2,1)S(1)}, u32[]{:S(2)}, u32[]{:S(2)}) collective-permute-start(bf16[64,1,2,256]{3,2,1,0:T(2,128)(2,1)S(1)} %get-tuple-element.276), channel_id=1, source_target_pairs={{2,0},{4,2},{6,4},{8,6},{10,8},{12,10},{14,12},{16,14},{18,16},{20... | collective-permute-start | bytes 196616 | tf_op jit(solution)/shard_map/ppermute | solution.py:17
  15.0 20.9 %collective-permute-start = (bf16[64,1,2,256]{3,2,1,0:T(2,128)(2,1)S(1)}, bf16[64,1,2,256]{3,2,1,0:T(2,128)(2,1)S(1)}, u32[]{:S(2)}, u32[]{:S(2)}) collective-permute-start(bf16[64,1,2,256]{3,2,1,0:T(2,128)(2,1)S(1)} %get-tuple-element.277), channel_id=1, source_target_pairs={{0,2},{2,4},{4,6},{6,8},{8,10},{10,12},{12,14},{14,16},{16,18},{18... | collective-permute-start | bytes 196616 | tf_op jit(solution)/shard_map/ppermute | solution.py:15
  19.4 16.6 %copy-start.17 = (bf16[64,2,2,256]{3,2,1,0:T(2,128)(2,1)S(1)}, bf16[64,2,2,256]{3,2,1,0:T(2,128)(2,1)}, u32[]{:S(2)}) copy-start(bf16[64,2,2,256]{3,2,1,0:T(2,128)(2,1)} %param.6) | copy-start | bytes 393220
  34.6 8.6 %copy-start.35 = (bf16[27,64,64]{2,1,0:T(8,128)(2,1)S(1)}, bf16[27,64,64]{2,1,0:T(8,128)(2,1)}, u32[]{:S(2)}) copy-start(bf16[27,64,64]{2,1,0:T(8,128)(2,1)} %param.7) | copy-start | bytes 663556
  37.6 32.6 %collective-permute-start.2 = (bf16[64,4,1,256]{3,2,1,0:T(2,128)(2,1)}, bf16[64,4,1,256]{3,2,1,0:T(2,128)(2,1)S(1)}, u32[]{:S(2)}, u32[]{:S(2)}) collective-permute-start(bf16[64,4,1,256]{3,2,1,0:T(2,128)(2,1)} %get-tuple-element.266), channel_id=1, source_target_pairs={{0,1},{2,3},{4,5},{6,7},{8,9},{10,11},{12,13},{14,15},{16,17},{18,... | collective-permute-start | bytes 393224 | tf_op jit(solution)/shard_map/ppermute | solution.py:15
  41.8 28.4 %collective-permute-start.3 = (bf16[64,4,1,256]{3,2,1,0:T(2,128)(2,1)}, bf16[64,4,1,256]{3,2,1,0:T(2,128)(2,1)S(1)}, u32[]{:S(2)}, u32[]{:S(2)}) collective-permute-start(bf16[64,4,1,256]{3,2,1,0:T(2,128)(2,1)} %get-tuple-element.267), channel_id=1, source_target_pairs={{1,0},{3,2},{5,4},{7,6},{9,8},{11,10},{13,12},{15,14},{17,16},{19,... | collective-permute-start | bytes 393224 | tf_op jit(solution)/shard_map/ppermute | solution.py:17
  45.4 12.1 %copy-start.67 = (bf16[64,3,64]{2,0,1:T(8,128)(2,1)S(1)}, bf16[64,3,64]{2,0,1:T(8,128)(2,1)}, u32[]{:S(2)}) copy-start(bf16[64,3,64]{2,0,1:T(8,128)(2,1)} %get-tuple-element.223) | copy-start | bytes 73732
  45.4 12.9 %copy-start.66 = (bf16[64,3,64]{2,0,1:T(8,128)(2,1)S(1)}, bf16[64,3,64]{2,0,1:T(8,128)(2,1)}, u32[]{:S(2)}) copy-start(bf16[64,3,64]{2,0,1:T(8,128)(2,1)} %get-tuple-element.224) | copy-start | bytes 73732
  45.4 13.6 %copy-start.65 = (bf16[64,3,64]{2,0,1:T(8,128)(2,1)S(1)}, bf16[64,3,64]{2,0,1:T(8,128)(2,1)}, u32[]{:S(2)}) copy-start(bf16[64,3,64]{2,0,1:T(8,128)(2,1)} %get-tuple-element.225) | copy-start | bytes 73732
  45.4 14.3 %copy-start.64 = (bf16[64,3,64]{2,0,1:T(8,128)(2,1)S(1)}, bf16[64,3,64]{2,0,1:T(8,128)(2,1)}, u32[]{:S(2)}) copy-start(bf16[64,3,64]{2,0,1:T(8,128)(2,1)} %get-tuple-element.226) | copy-start | bytes 73732
  45.4 15.0 %copy-start.63 = (bf16[64,3,64]{2,0,1:T(8,128)(2,1)S(1)}, bf16[64,3,64]{2,0,1:T(8,128)(2,1)}, u32[]{:S(2)}) copy-start(bf16[64,3,64]{2,0,1:T(8,128)(2,1)} %get-tuple-element.227) | copy-start | bytes 73732
  45.4 15.7 %copy-start.62 = (bf16[64,3,64]{2,0,1:T(8,128)(2,1)S(1)}, bf16[64,3,64]{2,0,1:T(8,128)(2,1)}, u32[]{:S(2)}) copy-start(bf16[64,3,64]{2,0,1:T(8,128)(2,1)} %get-tuple-element.228) | copy-start | bytes 73732
  45.4 16.4 %copy-start.61 = (bf16[64,3,64]{2,0,1:T(8,128)(2,1)S(1)}, bf16[64,3,64]{2,0,1:T(8,128)(2,1)}, u32[]{:S(2)}) copy-start(bf16[64,3,64]{2,0,1:T(8,128)(2,1)} %get-tuple-element.229) | copy-start | bytes 73732
  45.4 17.1 %copy-start.60 = (bf16[64,3,64]{2,0,1:T(8,128)(2,1)S(1)}, bf16[64,3,64]{2,0,1:T(8,128)(2,1)}, u32[]{:S(2)}) copy-start(bf16[64,3,64]{2,0,1:T(8,128)(2,1)} %get-tuple-element.230) | copy-start | bytes 73732
  45.4 17.8 %copy-start.59 = (bf16[64,3,64]{2,0,1:T(8,128)(2,1)S(1)}, bf16[64,3,64]{2,0,1:T(8,128)(2,1)}, u32[]{:S(2)}) copy-start(bf16[64,3,64]{2,0,1:T(8,128)(2,1)} %get-tuple-element.231) | copy-start | bytes 73732
  45.5 18.5 %copy-start.58 = (bf16[3,64,64]{2,1,0:T(8,128)(2,1)S(1)}, bf16[3,64,64]{2,1,0:T(8,128)(2,1)}, u32[]{:S(2)}) copy-start(bf16[3,64,64]{2,1,0:T(8,128)(2,1)} %get-tuple-element.232) | copy-start | bytes 73732
  45.5 19.1 %copy-start.57 = (bf16[3,64,64]{2,1,0:T(8,128)(2,1)S(1)}, bf16[3,64,64]{2,1,0:T(8,128)(2,1)}, u32[]{:S(2)}) copy-start(bf16[3,64,64]{2,1,0:T(8,128)(2,1)} %get-tuple-element.233) | copy-start | bytes 73732
  45.5 19.7 %copy-start.56 = (bf16[3,64,64]{2,1,0:T(8,128)(2,1)S(1)}, bf16[3,64,64]{2,1,0:T(8,128)(2,1)}, u32[]{:S(2)}) copy-start(bf16[3,64,64]{2,1,0:T(8,128)(2,1)} %get-tuple-element.234) | copy-start | bytes 73732
  45.5 20.3 %copy-start.55 = (bf16[3,64,64]{2,1,0:T(8,128)(2,1)S(1)}, bf16[3,64,64]{2,1,0:T(8,128)(2,1)}, u32[]{:S(2)}) copy-start(bf16[3,64,64]{2,1,0:T(8,128)(2,1)} %get-tuple-element.235) | copy-start | bytes 73732
  45.5 20.9 %copy-start.54 = (bf16[3,64,64]{2,1,0:T(8,128)(2,1)S(1)}, bf16[3,64,64]{2,1,0:T(8,128)(2,1)}, u32[]{:S(2)}) copy-start(bf16[3,64,64]{2,1,0:T(8,128)(2,1)} %get-tuple-element.236) | copy-start | bytes 73732
  45.5 21.5 %copy-start.53 = (bf16[3,64,64]{2,1,0:T(8,128)(2,1)S(1)}, bf16[3,64,64]{2,1,0:T(8,128)(2,1)}, u32[]{:S(2)}) copy-start(bf16[3,64,64]{2,1,0:T(8,128)(2,1)} %get-tuple-element.237) | copy-start | bytes 73732
  45.5 22.1 %copy-start.52 = (bf16[3,64,64]{2,1,0:T(8,128)(2,1)S(1)}, bf16[3,64,64]{2,1,0:T(8,128)(2,1)}, u32[]{:S(2)}) copy-start(bf16[3,64,64]{2,1,0:T(8,128)(2,1)} %get-tuple-element.238) | copy-start | bytes 73732
  45.5 22.8 %copy-start.51 = (bf16[3,64,64]{2,1,0:T(8,128)(2,1)S(1)}, bf16[3,64,64]{2,1,0:T(8,128)(2,1)}, u32[]{:S(2)}) copy-start(bf16[3,64,64]{2,1,0:T(8,128)(2,1)} %get-tuple-element.239) | copy-start | bytes 73732
  91.7 14.6 %copy-start.91 = (bf16[3,128,64]{1,2,0:T(8,128)(2,1)S(1)}, bf16[3,128,64]{1,2,0:T(8,128)(2,1)}, u32[]{:S(2)}) copy-start(bf16[3,128,64]{1,2,0:T(8,128)(2,1)} %copy.145) | copy-start | bytes 147460
  91.7 14.7 %copy-start.42 = (bf16[3,128,64]{1,2,0:T(8,128)(2,1)S(1)}, bf16[3,128,64]{1,2,0:T(8,128)(2,1)}, u32[]{:S(2)}) copy-start(bf16[3,128,64]{1,2,0:T(8,128)(2,1)} %copy.146) | copy-start | bytes 147460
  91.7 15.0 %copy-start.41 = (bf16[3,128,64]{1,2,0:T(8,128)(2,1)S(1)}, bf16[3,128,64]{1,2,0:T(8,128)(2,1)}, u32[]{:S(2)}) copy-start(bf16[3,128,64]{1,2,0:T(8,128)(2,1)} %copy.147) | copy-start | bytes 147460
  92.7 14.2 %copy-start.40 = (bf16[3,128,64]{1,2,0:T(8,128)(2,1)S(1)}, bf16[3,128,64]{1,2,0:T(8,128)(2,1)}, u32[]{:S(2)}) copy-start(bf16[3,128,64]{1,2,0:T(8,128)(2,1)} %copy.148) | copy-start | bytes 147460
  92.7 14.4 %copy-start.39 = (bf16[3,128,64]{1,2,0:T(8,128)(2,1)S(1)}, bf16[3,128,64]{1,2,0:T(8,128)(2,1)}, u32[]{:S(2)}) copy-start(bf16[3,128,64]{1,2,0:T(8,128)(2,1)} %copy.149) | copy-start | bytes 147460
  92.7 14.6 %copy-start.38 = (bf16[3,128,64]{1,2,0:T(8,128)(2,1)S(1)}, bf16[3,128,64]{1,2,0:T(8,128)(2,1)}, u32[]{:S(2)}) copy-start(bf16[3,128,64]{1,2,0:T(8,128)(2,1)} %copy.150) | copy-start | bytes 147460
  92.7 14.8 %copy-start.37 = (bf16[3,128,64]{1,2,0:T(8,128)(2,1)S(1)}, bf16[3,128,64]{1,2,0:T(8,128)(2,1)}, u32[]{:S(2)}) copy-start(bf16[3,128,64]{1,2,0:T(8,128)(2,1)} %copy.151) | copy-start | bytes 147460
  93.1 14.8 %copy-start.90 = (bf16[3,128,64]{1,2,0:T(8,128)(2,1)S(1)}, bf16[3,128,64]{1,2,0:T(8,128)(2,1)}, u32[]{:S(2)}) copy-start(bf16[3,128,64]{1,2,0:T(8,128)(2,1)} %copy.153) | copy-start | bytes 147460
  93.1 5.2 %collective-permute-start.5 = (bf16[64,1,1,128]{3,0,2,1:T(8,128)(2,1)S(1)}, bf16[64,1,1,128]{3,0,2,1:T(8,128)(2,1)S(1)}, u32[]{:S(2)}, u32[]{:S(2)}) collective-permute-start(bf16[64,1,1,128]{3,0,2,1:T(8,128)(2,1)S(1)} %fusion.245), channel_id=1, source_target_pairs={{2,0},{4,2},{6,4},{8,6},{10,8},{12,10},{14,12},{16,14},{18,16},{20... | collective-permute-start | bytes 49160 | tf_op jit(solution)/shard_map/ppermute | solution.py:17
  94.4 3.9 %collective-permute-start.4 = (bf16[64,1,1,128]{3,0,2,1:T(8,128)(2,1)S(1)}, bf16[64,1,1,128]{3,0,2,1:T(8,128)(2,1)S(1)}, u32[]{:S(2)}, u32[]{:S(2)}) collective-permute-start(bf16[64,1,1,128]{3,0,2,1:T(8,128)(2,1)S(1)} %fusion.245), channel_id=1, source_target_pairs={{0,2},{2,4},{4,6},{6,8},{8,10},{10,12},{12,14},{14,16},{16,18},{18... | collective-permute-start | bytes 49160 | tf_op jit(solution)/shard_map/ppermute | solution.py:15
  98.4 6.1 %collective-permute-start.7 = (bf16[64,3,1,128]{3,0,2,1:T(8,128)(2,1)S(1)}, bf16[64,3,1,128]{3,0,2,1:T(8,128)(2,1)S(1)}, u32[]{:S(2)}, u32[]{:S(2)}) collective-permute-start(bf16[64,3,1,128]{3,0,2,1:T(8,128)(2,1)S(1)} %pad_maximum_fusion.18), channel_id=1, source_target_pairs={{1,0},{3,2},{5,4},{7,6},{9,8},{11,10},{13,12},{15,14},{17,16},{19,... | collective-permute-start | bytes 147464 | tf_op jit(solution)/shard_map/ppermute | solution.py:17
  99.7 6.3 %collective-permute-start.6 = (bf16[64,3,1,128]{3,0,2,1:T(8,128)(2,1)S(1)}, bf16[64,3,1,128]{3,0,2,1:T(8,128)(2,1)S(1)}, u32[]{:S(2)}, u32[]{:S(2)}) collective-permute-start(bf16[64,3,1,128]{3,0,2,1:T(8,128)(2,1)S(1)} %pad_maximum_fusion.18), channel_id=1, source_target_pairs={{0,1},{2,3},{4,5},{6,7},{8,9},{10,11},{12,13},{14,15},{16,17},{18,... | collective-permute-start | bytes 147464 | tf_op jit(solution)/shard_map/ppermute | solution.py:15
  106.7 8.5 %copy-start.78 = (bf16[64,128]{1,0:T(8,128)(2,1)}, bf16[64,128]{1,0:T(8,128)(2,1)S(1)}, u32[]{:S(2)}) copy-start(bf16[64,128]{1,0:T(8,128)(2,1)S(1)} %get-tuple-element.280) | copy-start | bytes 49156
  108.2 20.6 %collective-permute-start.9 = (bf16[128,1,1,128]{0,3,2,1:T(8,128)(2,1)S(1)}, bf16[128,1,1,128]{0,3,2,1:T(8,128)(2,1)S(1)}, u32[]{:S(2)}, u32[]{:S(2)}) collective-permute-start(bf16[128,1,1,128]{0,3,2,1:T(8,128)(2,1)S(1)} %bitcast.408), channel_id=1, source_target_pairs={{2,0},{4,2},{6,4},{8,6},{10,8},{12,10},{14,12},{16,14},{18,16},{20... | collective-permute-start | bytes 98312 | tf_op jit(solution)/shard_map/ppermute | solution.py:17
  109.5 19.3 %collective-permute-start.8 = (bf16[128,1,1,128]{0,3,2,1:T(8,128)(2,1)S(1)}, bf16[128,1,1,128]{0,3,2,1:T(8,128)(2,1)S(1)}, u32[]{:S(2)}, u32[]{:S(2)}) collective-permute-start(bf16[128,1,1,128]{0,3,2,1:T(8,128)(2,1)S(1)} %bitcast.409), channel_id=1, source_target_pairs={{0,2},{2,4},{4,6},{6,8},{8,10},{10,12},{12,14},{14,16},{16,18},{18... | collective-permute-start | bytes 98312 | tf_op jit(solution)/shard_map/ppermute | solution.py:15
  115.9 18.9 %all-to-all-start = ((bf16[2,2,4096]{2,1,0:T(2,128)(2,1)}), bf16[2,2,4096]{2,1,0:T(2,128)(2,1)S(1)}, u32[]{:S(2)}, u32[]{:S(2)}) async-start(bf16[2,2,4096]{2,1,0:T(2,128)(2,1)} %reshape.942), calls=%async_computation | async-start | bytes 65536 | tf_op jit(solution)/shard_map/all_to_all | solution.py:129
  119.2 187.0 %all-reduce.7.cloned.1.call-start = ((), (), s32[]{:S(2)}) async-start(), calls=%async_computation.2 | async-start | bytes 5308416 | tf_op jit(solution)/shard_map/psum | solution.py:155
  128.8 6.7 %collective-permute-start.11 = (bf16[128,3,1,128]{0,3,2,1:T(8,128)(2,1)S(1)}, bf16[128,3,1,128]{0,3,2,1:T(8,128)(2,1)S(1)}, u32[]{:S(2)}, u32[]{:S(2)}) collective-permute-start(bf16[128,3,1,128]{0,3,2,1:T(8,128)(2,1)S(1)} %pad_maximum_fusion.17), channel_id=1, source_target_pairs={{1,0},{3,2},{5,4},{7,6},{9,8},{11,10},{13,12},{15,14},{17,16},{19,... | collective-permute-start | bytes 294920 | tf_op jit(solution)/shard_map/ppermute | solution.py:17
  130.1 6.8 %collective-permute-start.10 = (bf16[128,3,1,128]{0,3,2,1:T(8,128)(2,1)S(1)}, bf16[128,3,1,128]{0,3,2,1:T(8,128)(2,1)S(1)}, u32[]{:S(2)}, u32[]{:S(2)}) collective-permute-start(bf16[128,3,1,128]{0,3,2,1:T(8,128)(2,1)S(1)} %pad_maximum_fusion.17), channel_id=1, source_target_pairs={{0,1},{2,3},{4,5},{6,7},{8,9},{10,11},{12,13},{14,15},{16,17},{18,... | collective-permute-start | bytes 294920 | tf_op jit(solution)/shard_map/ppermute | solution.py:15
  137.4 6.9 %copy-start.36 = (f32[64,1024]{1,0:T(8,128)S(1)}, f32[64,1024]{1,0:T(8,128)}, u32[]{:S(2)}) copy-start(f32[64,1024]{1,0:T(8,128)} %get-tuple-element.287) | copy-start | bytes 786436
  147.0 6.7 %collective-permute-start.13 = (bf16[64,1,2,256]{3,2,1,0:T(2,128)(2,1)S(1)}, bf16[64,1,2,256]{3,2,1,0:T(2,128)(2,1)S(1)}, u32[]{:S(2)}, u32[]{:S(2)}) collective-permute-start(bf16[64,1,2,256]{3,2,1,0:T(2,128)(2,1)S(1)} %get-tuple-element.271), channel_id=1, source_target_pairs={{2,0},{4,2},{6,4},{8,6},{10,8},{12,10},{14,12},{16,14},{18,16},{20... | collective-permute-start | bytes 196616 | tf_op jit(solution)/shard_map/ppermute | solution.py:17
  148.3 5.4 %collective-permute-start.12 = (bf16[64,1,2,256]{3,2,1,0:T(2,128)(2,1)S(1)}, bf16[64,1,2,256]{3,2,1,0:T(2,128)(2,1)S(1)}, u32[]{:S(2)}, u32[]{:S(2)}) collective-permute-start(bf16[64,1,2,256]{3,2,1,0:T(2,128)(2,1)S(1)} %get-tuple-element.272), channel_id=1, source_target_pairs={{0,2},{2,4},{4,6},{6,8},{8,10},{10,12},{12,14},{14,16},{16,18},{18... | collective-permute-start | bytes 196616 | tf_op jit(solution)/shard_map/ppermute | solution.py:15
  154.6 9.0 %collective-permute-start.14 = (bf16[64,4,1,256]{3,2,1,0:T(2,128)(2,1)S(1)}, bf16[64,4,1,256]{3,2,1,0:T(2,128)(2,1)S(1)}, u32[]{:S(2)}, u32[]{:S(2)}) collective-permute-start(bf16[64,4,1,256]{3,2,1,0:T(2,128)(2,1)S(1)} %get-tuple-element.261), channel_id=1, source_target_pairs={{0,1},{2,3},{4,5},{6,7},{8,9},{10,11},{12,13},{14,15},{16,17},{18,... | collective-permute-start | bytes 393224 | tf_op jit(solution)/shard_map/ppermute | solution.py:15
  158.6 9.7 %collective-permute-start.15 = (bf16[64,4,1,256]{3,2,1,0:T(2,128)(2,1)S(1)}, bf16[64,4,1,256]{3,2,1,0:T(2,128)(2,1)S(1)}, u32[]{:S(2)}, u32[]{:S(2)}) collective-permute-start(bf16[64,4,1,256]{3,2,1,0:T(2,128)(2,1)S(1)} %get-tuple-element.262), channel_id=1, source_target_pairs={{1,0},{3,2},{5,4},{7,6},{9,8},{11,10},{13,12},{15,14},{17,16},{19,... | collective-permute-start | bytes 393224 | tf_op jit(solution)/shard_map/ppermute | solution.py:17
  (66 other events, 129.1 us)
Sparse Core Ops, SparseCore 0:
  161.2 144.9 all-reduce.6
where the time goes:
time: 318 us; the launch traced here: 317 us
  waiting for transfers between devices  131 us (41%)
  local copies, waits for them, and re-layouts  75.2 us (24%)
  starting transfers between devices  49.8 us (16%)
  between operations  16.3 us (5%)
  blocking collectives  15.2 us (5%)
  matrix products  14.6 us (5%)
  other arithmetic  14.5 us (5%)
    psum x1, waiting for transfers between devices, local(): lax.psum(conv_weights(first_down, padded_in, fine_shape), ('space', 'filt'))  120 us
    ppermute x8, starting transfers between devices, extended(): lax.ppermute(tail, axis, [(i, (i + 1) % count) for i in range(ends)])  31.4 us
    unnamed x237, local copies, waits for them, and re-layouts  25.8 us
    reshape x58, local copies, waits for them, and re-layouts, window(): return section.reshape(padded.shape[0], extent_x * extent_y * extent_z)  17.6 us
    all_gather x1, blocking collectives, local(): whole_weight = lax.all_gather(second_weight, 'filt', axis=1, tiled=True)  15.2 us
    ppermute x8, starting transfers between devices, extended(): lax.ppermute(head, axis, [((i + 1) % count, i) for i in range(ends)])  10.8 us
    concatenate x10, other arithmetic, extended(): jnp.concatenate([lax.ppermute(tail, axis, [(i, (i + 1) % count) for i in...  9.21 us
    rev x27, local copies, waits for them, and re-layouts, conv_transpose(): tap_block = weight[24 - tap_base:27 - tap_base][::-1]  6.46 us
  transfers between devices with their start and end apart: 19, of which 6 were waited for; matrix products, arithmetic and copies ran while one was open for 27% of the time, Pallas kernels for 0%

commit v1 on v0

--- a/solution.py
+++ b/solution.py
@@ -152,7 +152,8 @@
     hidden_grad = spread_cells(pool_grad.reshape((channels,) + brick_shape))
     first_down = (hidden_grad.reshape(channels, -1) * silu_slope(first_pre)).astype(jnp.bfloat16)
     first_grad = (
-        lax.psum(conv_weights(first_down, padded_in, fine_shape), ("space", "filt")) * fine_scale
+        lax.psum(lax.psum(conv_weights(first_down, padded_in, fine_shape), "space"), "filt")
+        * fine_scale
     )
     padded_back = pad_depth(
         extended(first_down.reshape((channels,) + fine_shape), (("space", 1), ("filt", 2)), 1)

time: 318 us -> 450 us (1.42)
  waiting for transfers between devices: 131 us -> 252 us
    psum x1 -> x3, waiting for transfers between devices: 120 us -> 243 us  [the longest x1 136 us: local(): lax.psum(conv_weights(down_grad, padded_pool, brick_shape), ('space', 'fi...]
    unnamed x237 -> x219, local copies, waits for them, and re-layouts: 25.8 us -> 24.7 us
  transfers between devices with their start and end apart: 19 -> 21, of which waited for: 6 -> 7; matrix products, arithmetic and copies ran while one was open for 27% -> 23% of each run, Pallas kernels for 0% -> 0%
where the time goes in v1:
time: 450 us; the launch traced here: 448 us
  waiting for transfers between devices  252 us (56%)
  local copies, waits for them, and re-layouts  77.8 us (17%)
  starting transfers between devices  50.5 us (11%)
  other arithmetic  18.1 us (4%)
  matrix products  18.1 us (4%)
  between operations  16 us (4%)
  blocking collectives  15.2 us (3%)
    psum x1, waiting for transfers between devices, local(): lax.psum(conv_weights(down_grad, padded_pool, brick_shape), ('space', 'fi...  136 us
    psum x1, waiting for transfers between devices, local(): lax.psum(conv_weights(first_down, padded_in, fine_shape), 'space')  70.8 us
    psum x1, waiting for transfers between devices, local(): lax.psum(lax.psum(conv_weights(first_down, padded_in, fine_shape), 'space...  36.4 us
    ppermute x8, starting transfers between devices, extended(): lax.ppermute(tail, axis, [(i, (i + 1) % count) for i in range(ends)])  31.5 us
    unnamed x219, local copies, waits for them, and re-layouts  24.7 us
    reshape x58, local copies, waits for them, and re-layouts, window(): return section.reshape(padded.shape[0], extent_x * extent_y * extent_z)  17.6 us
    all_gather x1, blocking collectives, local(): whole_weight = lax.all_gather(second_weight, 'filt', axis=1, tiled=True)  15.2 us
    concatenate x10, other arithmetic, extended(): jnp.concatenate([lax.ppermute(tail, axis, [(i, (i + 1) % count) for i in...  10.7 us
  transfers between devices with their start and end apart: 21, of which 7 were waited for; matrix products, arithmetic and copies ran while one was open for 23% of the time, Pallas kernels for 0%

profile of v1, /device:TPU:0, one launch (start us, length us, event | category | flops | bytes accessed | tf_op | source)
XLA Modules:
  0.0 447.9 jit_solution(2193131205420616696)
XLA Ops:
  7.2 1.4 copy.107
  8.5 4.2 all-to-all-start.1
  13.7 1.3 collective-permute-start.1
  15.0 3.0 collective-permute-start
  18.1 1.3 copy.96
  19.4 15.2 %all_gather.3 = bf16[27,128,64]{2,0,1:T(8,128)(2,1)S(1)} all-gather(bf16[27,64,64]{2,0,1:T(8,128)(2,1)S(1)} %copy.96), channel_id=1, replica_groups=mesh['space'=16,'filt'=2] {'filt'}, dimensions={1}, use_global_device_ids=true | all-gather | bytes 663552 | tf_op jit(solution)/shard_map/all_gather | solution.py:124
  34.6 1.3 fusion.155
  37.6 4.2 collective-permute-start.2
  41.8 1.5 collective-permute-start.3
  45.5 1.8 copy.153
  48.3 1.6 copy.151
  50.0 1.6 copy.150
  51.6 1.6 copy.149
  56.1 1.4 rev.98
  70.3 1.7 pad_maximum_fusion.9
  75.7 2.4 select_maximum_fusion.2
  78.1 2.9 fusion.157
  91.1 1.2 fusion.163
  96.7 1.3 collective-permute-start.5
  98.0 3.0 collective-permute-start.4
  102.0 1.3 collective-permute-start.7
  103.3 4.8 %collective-permute-start.6 = (bf16[64,3,1,128]{3,0,2,1:T(8,128)(2,1)S(1)}, bf16[64,3,1,128]{3,0,2,1:T(8,128)(2,1)S(1)}, u32[]{:S(2)}, u32[]{:S(2)}) collective-permute-start(bf16[64,3,1,128]{3,0,2,1:T(8,128)(2,1)S(1)} %pad_maximum_fusion.18), channel_id=1, source_target_pairs={{0,1},{2,3},{4,5},{6,7},{8,9},{10,11},{12,13},{14,15},{16,17},{18,... | collective-permute-start | bytes 147464 | tf_op jit(solution)/shard_map/ppermute | solution.py:15
  108.1 1.5 collective-permute-done.6
  111.8 1.3 collective-permute-start.9
  113.1 3.9 collective-permute-start.8
  122.6 3.9 all-to-all-start
  128.1 1.7 copy.125
  129.8 1.7 copy.124
  131.5 1.7 copy.123
  138.2 1.3 collective-permute-start.11
  139.5 4.6 %collective-permute-start.10 = (bf16[128,3,1,128]{0,3,2,1:T(8,128)(2,1)S(1)}, bf16[128,3,1,128]{0,3,2,1:T(8,128)(2,1)S(1)}, u32[]{:S(2)}, u32[]{:S(2)}) collective-permute-start(bf16[128,3,1,128]{0,3,2,1:T(8,128)(2,1)S(1)} %pad_maximum_fusion.17), channel_id=1, source_target_pairs={{0,1},{2,3},{4,5},{6,7},{8,9},{10,11},{12,13},{14,15},{16,17},{18,... | collective-permute-start | bytes 294920 | tf_op jit(solution)/shard_map/ppermute | solution.py:15
  145.1 1.2 collective-permute-done.10
  147.5 5.5 %while.14 = (s32[]{:T(128)}, f32[64,128]{1,0:T(8,128)}, bf16[27,128,64]{2,1,0:T(8,128)(2,1)S(1)}, bf16[128,3,3,130]{3,0,2,1:T(8,128)(2,1)S(1)}, s32[]{:T(128)}, ...) while((s32[]{:T(128)}, f32[64,128]{1,0:T(8,128)}, ...), condition=%wide.region_2.3_spmd.clone, body=%wide.region_1.2_spmd.clone.sunk | while | flops 29736976 | bytes 3318213 | solution.py:149
  157.9 1.3 collective-permute-start.13
  159.2 3.9 collective-permute-start.12
  165.2 4.0 collective-permute-start.14
  169.2 1.3 collective-permute-start.15
  173.2 1.6 collective-permute-done.14
  174.8 4.7 %collective-permute-done.15 = bf16[64,4,1,256]{3,2,1,0:T(2,128)(2,1)S(1)} collective-permute-done((bf16[64,4,1,256]{3,2,1,0:T(2,128)(2,1)S(1)}, bf16[64,4,1,256]{3,2,1,0:T(2,128)(2,1)S(1)}, u32[]{:S(2)}, u32[]{:S(2)}) %collective-permute-start.15) | collective-permute-done | bytes 131104 | tf_op jit(solution)/shard_map/ppermute | solution.py:17
  179.5 1.7 pad_maximum_fusion.1
  182.9 2.4 select_maximum_fusion
  185.3 2.9 fusion.156
  192.3 70.8 %all-reduce.8.cloned.1.call-done = f32[27,64,64]{1,2,0:T(8,128)} async-done(((f32[27,64,64]{1,2,0:T(8,128)}), f32[27,64,64]{1,2,0:T(8,128)}) %all-reduce.8.cloned.1.call-update) | async-done | bytes 442384 | tf_op jit(solution)/shard_map/psum | solution.py:155
  264.6 135.7 %all-reduce.12.cloned.1.call-done = f32[27,128,64]{2,1,0:T(8,128)} async-done(((f32[27,128,64]{2,1,0:T(8,128)}), f32[27,128,64]{2,1,0:T(8,128)}) %all-reduce.12.cloned.1.call-update) | async-done | bytes 884752 | tf_op jit(solution)/shard_map/psum | solution.py:134
  400.3 2.2 dynamic-slice_multiply_fusion
  402.4 36.4 %all-reduce.10.cloned.1.call-done = f32[27,64,64]{1,2,0:T(8,128)} async-done(((f32[27,64,64]{1,2,0:T(8,128)}), f32[27,64,64]{1,2,0:T(8,128)}) %all-reduce.10.cloned.1.call-update) | async-done | bytes 442384 | tf_op jit(solution)/shard_map/psum | solution.py:155
  438.9 1.3 broadcast_multiply_fusion
  440.2 1.2 copy.133
  (447 shorter events, 77.3 us)
Async XLA Ops:
  8.5 92.5 %all-to-all-start.1 = ((bf16[64,1,2,128]{3,0,1,2:T(8,128)(2,1)}), bf16[64,1,2,128]{3,0,1,2:T(8,128)(2,1)}, u32[]{:S(2)}, u32[]{:S(2)}) async-start(bf16[64,1,2,128]{3,0,1,2:T(8,128)(2,1)} %copy.107), calls=%async_computation.1 | async-start | bytes 65536 | tf_op jit(solution)/shard_map/all_to_all | solution.py:130
  13.7 22.2 %collective-permute-start.1 = (bf16[64,1,2,256]{3,2,1,0:T(2,128)(2,1)S(1)}, bf16[64,1,2,256]{3,2,1,0:T(2,128)(2,1)S(1)}, u32[]{:S(2)}, u32[]{:S(2)}) collective-permute-start(bf16[64,1,2,256]{3,2,1,0:T(2,128)(2,1)S(1)} %get-tuple-element.274), channel_id=1, source_target_pairs={{2,0},{4,2},{6,4},{8,6},{10,8},{12,10},{14,12},{16,14},{18,16},{20... | collective-permute-start | bytes 196616 | tf_op jit(solution)/shard_map/ppermute | solution.py:17
  15.0 20.9 %collective-permute-start = (bf16[64,1,2,256]{3,2,1,0:T(2,128)(2,1)S(1)}, bf16[64,1,2,256]{3,2,1,0:T(2,128)(2,1)S(1)}, u32[]{:S(2)}, u32[]{:S(2)}) collective-permute-start(bf16[64,1,2,256]{3,2,1,0:T(2,128)(2,1)S(1)} %get-tuple-element.275), channel_id=1, source_target_pairs={{0,2},{2,4},{4,6},{6,8},{8,10},{10,12},{12,14},{14,16},{16,18},{18... | collective-permute-start | bytes 196616 | tf_op jit(solution)/shard_map/ppermute | solution.py:15
  19.4 16.6 %copy-start.9 = (bf16[64,2,2,256]{3,2,1,0:T(2,128)(2,1)S(1)}, bf16[64,2,2,256]{3,2,1,0:T(2,128)(2,1)}, u32[]{:S(2)}) copy-start(bf16[64,2,2,256]{3,2,1,0:T(2,128)(2,1)} %param.6) | copy-start | bytes 393220
  37.6 32.7 %collective-permute-start.2 = (bf16[64,4,1,256]{3,2,1,0:T(2,128)(2,1)}, bf16[64,4,1,256]{3,2,1,0:T(2,128)(2,1)S(1)}, u32[]{:S(2)}, u32[]{:S(2)}) collective-permute-start(bf16[64,4,1,256]{3,2,1,0:T(2,128)(2,1)} %get-tuple-element.264), channel_id=1, source_target_pairs={{0,1},{2,3},{4,5},{6,7},{8,9},{10,11},{12,13},{14,15},{16,17},{18,... | collective-permute-start | bytes 393224 | tf_op jit(solution)/shard_map/ppermute | solution.py:15
  41.8 28.5 %collective-permute-start.3 = (bf16[64,4,1,256]{3,2,1,0:T(2,128)(2,1)}, bf16[64,4,1,256]{3,2,1,0:T(2,128)(2,1)S(1)}, u32[]{:S(2)}, u32[]{:S(2)}) collective-permute-start(bf16[64,4,1,256]{3,2,1,0:T(2,128)(2,1)} %get-tuple-element.265), channel_id=1, source_target_pairs={{1,0},{3,2},{5,4},{7,6},{9,8},{11,10},{13,12},{15,14},{17,16},{19,... | collective-permute-start | bytes 393224 | tf_op jit(solution)/shard_map/ppermute | solution.py:17
  45.4 12.9 %copy-start.62 = (bf16[64,3,64]{2,0,1:T(8,128)(2,1)S(1)}, bf16[64,3,64]{2,0,1:T(8,128)(2,1)}, u32[]{:S(2)}) copy-start(bf16[64,3,64]{2,0,1:T(8,128)(2,1)} %get-tuple-element.222) | copy-start | bytes 73732
  45.4 13.6 %copy-start.61 = (bf16[64,3,64]{2,0,1:T(8,128)(2,1)S(1)}, bf16[64,3,64]{2,0,1:T(8,128)(2,1)}, u32[]{:S(2)}) copy-start(bf16[64,3,64]{2,0,1:T(8,128)(2,1)} %get-tuple-element.223) | copy-start | bytes 73732
  45.4 14.3 %copy-start.60 = (bf16[64,3,64]{2,0,1:T(8,128)(2,1)S(1)}, bf16[64,3,64]{2,0,1:T(8,128)(2,1)}, u32[]{:S(2)}) copy-start(bf16[64,3,64]{2,0,1:T(8,128)(2,1)} %get-tuple-element.224) | copy-start | bytes 73732
  45.4 15.0 %copy-start.59 = (bf16[64,3,64]{2,0,1:T(8,128)(2,1)S(1)}, bf16[64,3,64]{2,0,1:T(8,128)(2,1)}, u32[]{:S(2)}) copy-start(bf16[64,3,64]{2,0,1:T(8,128)(2,1)} %get-tuple-element.225) | copy-start | bytes 73732
  45.4 15.7 %copy-start.58 = (bf16[64,3,64]{2,0,1:T(8,128)(2,1)S(1)}, bf16[64,3,64]{2,0,1:T(8,128)(2,1)}, u32[]{:S(2)}) copy-start(bf16[64,3,64]{2,0,1:T(8,128)(2,1)} %get-tuple-element.226) | copy-start | bytes 73732
  45.4 16.4 %copy-start.57 = (bf16[64,3,64]{2,0,1:T(8,128)(2,1)S(1)}, bf16[64,3,64]{2,0,1:T(8,128)(2,1)}, u32[]{:S(2)}) copy-start(bf16[64,3,64]{2,0,1:T(8,128)(2,1)} %get-tuple-element.227) | copy-start | bytes 73732
  45.4 17.1 %copy-start.56 = (bf16[64,3,64]{2,0,1:T(8,128)(2,1)S(1)}, bf16[64,3,64]{2,0,1:T(8,128)(2,1)}, u32[]{:S(2)}) copy-start(bf16[64,3,64]{2,0,1:T(8,128)(2,1)} %get-tuple-element.228) | copy-start | bytes 73732
  45.4 17.8 %copy-start.55 = (bf16[64,3,64]{2,0,1:T(8,128)(2,1)S(1)}, bf16[64,3,64]{2,0,1:T(8,128)(2,1)}, u32[]{:S(2)}) copy-start(bf16[64,3,64]{2,0,1:T(8,128)(2,1)} %get-tuple-element.229) | copy-start | bytes 73732
  45.4 18.5 %copy-start.54 = (bf16[3,64,64]{2,1,0:T(8,128)(2,1)S(1)}, bf16[3,64,64]{2,1,0:T(8,128)(2,1)}, u32[]{:S(2)}) copy-start(bf16[3,64,64]{2,1,0:T(8,128)(2,1)} %get-tuple-element.230) | copy-start | bytes 73732
  45.5 19.1 %copy-start.53 = (bf16[3,64,64]{2,1,0:T(8,128)(2,1)S(1)}, bf16[3,64,64]{2,1,0:T(8,128)(2,1)}, u32[]{:S(2)}) copy-start(bf16[3,64,64]{2,1,0:T(8,128)(2,1)} %get-tuple-element.231) | copy-start | bytes 73732
  45.5 19.7 %copy-start.52 = (bf16[3,64,64]{2,1,0:T(8,128)(2,1)S(1)}, bf16[3,64,64]{2,1,0:T(8,128)(2,1)}, u32[]{:S(2)}) copy-start(bf16[3,64,64]{2,1,0:T(8,128)(2,1)} %get-tuple-element.232) | copy-start | bytes 73732
  45.5 20.3 %copy-start.51 = (bf16[3,64,64]{2,1,0:T(8,128)(2,1)S(1)}, bf16[3,64,64]{2,1,0:T(8,128)(2,1)}, u32[]{:S(2)}) copy-start(bf16[3,64,64]{2,1,0:T(8,128)(2,1)} %get-tuple-element.233) | copy-start | bytes 73732
  45.5 20.9 %copy-start.50 = (bf16[3,64,64]{2,1,0:T(8,128)(2,1)S(1)}, bf16[3,64,64]{2,1,0:T(8,128)(2,1)}, u32[]{:S(2)}) copy-start(bf16[3,64,64]{2,1,0:T(8,128)(2,1)} %get-tuple-element.234) | copy-start | bytes 73732
  45.5 21.5 %copy-start.49 = (bf16[3,64,64]{2,1,0:T(8,128)(2,1)S(1)}, bf16[3,64,64]{2,1,0:T(8,128)(2,1)}, u32[]{:S(2)}) copy-start(bf16[3,64,64]{2,1,0:T(8,128)(2,1)} %get-tuple-element.235) | copy-start | bytes 73732
  45.5 22.2 %copy-start.48 = (bf16[3,64,64]{2,1,0:T(8,128)(2,1)S(1)}, bf16[3,64,64]{2,1,0:T(8,128)(2,1)}, u32[]{:S(2)}) copy-start(bf16[3,64,64]{2,1,0:T(8,128)(2,1)} %get-tuple-element.236) | copy-start | bytes 73732
  45.5 22.8 %copy-start.47 = (bf16[3,64,64]{2,1,0:T(8,128)(2,1)S(1)}, bf16[3,64,64]{2,1,0:T(8,128)(2,1)}, u32[]{:S(2)}) copy-start(bf16[3,64,64]{2,1,0:T(8,128)(2,1)} %get-tuple-element.237) | copy-start | bytes 73732
  95.3 14.6 %copy-start.82 = (bf16[3,128,64]{1,2,0:T(8,128)(2,1)S(1)}, bf16[3,128,64]{1,2,0:T(8,128)(2,1)}, u32[]{:S(2)}) copy-start(bf16[3,128,64]{1,2,0:T(8,128)(2,1)} %copy.145) | copy-start | bytes 147460
  95.3 14.7 %copy-start.39 = (bf16[3,128,64]{1,2,0:T(8,128)(2,1)S(1)}, bf16[3,128,64]{1,2,0:T(8,128)(2,1)}, u32[]{:S(2)}) copy-start(bf16[3,128,64]{1,2,0:T(8,128)(2,1)} %copy.146) | copy-start | bytes 147460
  95.4 15.0 %copy-start.38 = (bf16[3,128,64]{1,2,0:T(8,128)(2,1)S(1)}, bf16[3,128,64]{1,2,0:T(8,128)(2,1)}, u32[]{:S(2)}) copy-start(bf16[3,128,64]{1,2,0:T(8,128)(2,1)} %copy.147) | copy-start | bytes 147460
  96.3 14.2 %copy-start.37 = (bf16[3,128,64]{1,2,0:T(8,128)(2,1)S(1)}, bf16[3,128,64]{1,2,0:T(8,128)(2,1)}, u32[]{:S(2)}) copy-start(bf16[3,128,64]{1,2,0:T(8,128)(2,1)} %copy.148) | copy-start | bytes 147460
  96.3 14.4 %copy-start.36 = (bf16[3,128,64]{1,2,0:T(8,128)(2,1)S(1)}, bf16[3,128,64]{1,2,0:T(8,128)(2,1)}, u32[]{:S(2)}) copy-start(bf16[3,128,64]{1,2,0:T(8,128)(2,1)} %copy.149) | copy-start | bytes 147460
  96.3 14.6 %copy-start.35 = (bf16[3,128,64]{1,2,0:T(8,128)(2,1)S(1)}, bf16[3,128,64]{1,2,0:T(8,128)(2,1)}, u32[]{:S(2)}) copy-start(bf16[3,128,64]{1,2,0:T(8,128)(2,1)} %copy.150) | copy-start | bytes 147460
  96.3 14.8 %copy-start.34 = (bf16[3,128,64]{1,2,0:T(8,128)(2,1)S(1)}, bf16[3,128,64]{1,2,0:T(8,128)(2,1)}, u32[]{:S(2)}) copy-start(bf16[3,128,64]{1,2,0:T(8,128)(2,1)} %copy.151) | copy-start | bytes 147460
  96.7 14.8 %copy-start.81 = (bf16[3,128,64]{1,2,0:T(8,128)(2,1)S(1)}, bf16[3,128,64]{1,2,0:T(8,128)(2,1)}, u32[]{:S(2)}) copy-start(bf16[3,128,64]{1,2,0:T(8,128)(2,1)} %copy.153) | copy-start | bytes 147460
  96.7 5.2 %collective-permute-start.5 = (bf16[64,1,1,128]{3,0,2,1:T(8,128)(2,1)S(1)}, bf16[64,1,1,128]{3,0,2,1:T(8,128)(2,1)S(1)}, u32[]{:S(2)}, u32[]{:S(2)}) collective-permute-start(bf16[64,1,1,128]{3,0,2,1:T(8,128)(2,1)S(1)} %fusion.245), channel_id=1, source_target_pairs={{2,0},{4,2},{6,4},{8,6},{10,8},{12,10},{14,12},{16,14},{18,16},{20... | collective-permute-start | bytes 49160 | tf_op jit(solution)/shard_map/ppermute | solution.py:17
  98.0 3.9 collective-permute-start.4
  102.0 6.1 %collective-permute-start.7 = (bf16[64,3,1,128]{3,0,2,1:T(8,128)(2,1)S(1)}, bf16[64,3,1,128]{3,0,2,1:T(8,128)(2,1)S(1)}, u32[]{:S(2)}, u32[]{:S(2)}) collective-permute-start(bf16[64,3,1,128]{3,0,2,1:T(8,128)(2,1)S(1)} %pad_maximum_fusion.18), channel_id=1, source_target_pairs={{1,0},{3,2},{5,4},{7,6},{9,8},{11,10},{13,12},{15,14},{17,16},{19,... | collective-permute-start | bytes 147464 | tf_op jit(solution)/shard_map/ppermute | solution.py:17
  103.3 6.3 %collective-permute-start.6 = (bf16[64,3,1,128]{3,0,2,1:T(8,128)(2,1)S(1)}, bf16[64,3,1,128]{3,0,2,1:T(8,128)(2,1)S(1)}, u32[]{:S(2)}, u32[]{:S(2)}) collective-permute-start(bf16[64,3,1,128]{3,0,2,1:T(8,128)(2,1)S(1)} %pad_maximum_fusion.18), channel_id=1, source_target_pairs={{0,1},{2,3},{4,5},{6,7},{8,9},{10,11},{12,13},{14,15},{16,17},{18,... | collective-permute-start | bytes 147464 | tf_op jit(solution)/shard_map/ppermute | solution.py:15
  111.8 24.5 %collective-permute-start.9 = (bf16[128,1,1,128]{0,3,2,1:T(8,128)(2,1)S(1)}, bf16[128,1,1,128]{0,3,2,1:T(8,128)(2,1)S(1)}, u32[]{:S(2)}, u32[]{:S(2)}) collective-permute-start(bf16[128,1,1,128]{0,3,2,1:T(8,128)(2,1)S(1)} %bitcast.408), channel_id=1, source_target_pairs={{2,0},{4,2},{6,4},{8,6},{10,8},{12,10},{14,12},{16,14},{18,16},{20... | collective-permute-start | bytes 98312 | tf_op jit(solution)/shard_map/ppermute | solution.py:17
  113.1 23.2 %collective-permute-start.8 = (bf16[128,1,1,128]{0,3,2,1:T(8,128)(2,1)S(1)}, bf16[128,1,1,128]{0,3,2,1:T(8,128)(2,1)}, u32[]{:S(2)}, u32[]{:S(2)}) collective-permute-start(bf16[128,1,1,128]{0,3,2,1:T(8,128)(2,1)S(1)} %bitcast.409), channel_id=1, source_target_pairs={{0,2},{2,4},{4,6},{6,8},{8,10},{10,12},{12,14},{14,16},{16,18},{18... | collective-permute-start | bytes 98312 | tf_op jit(solution)/shard_map/ppermute | solution.py:15
  122.6 48.9 %all-to-all-start = ((bf16[2,2,4096]{2,1,0:T(2,128)(2,1)}), bf16[2,2,4096]{2,1,0:T(2,128)(2,1)}, u32[]{:S(2)}, u32[]{:S(2)}) async-start(bf16[2,2,4096]{2,1,0:T(2,128)(2,1)} %reshape.942), calls=%async_computation | async-start | bytes 65536 | tf_op jit(solution)/shard_map/all_to_all | solution.py:129
  126.5 136.6 %all-reduce.8.cloned.1.call-start = ((), (), s32[]{:S(2)}) async-start(), calls=%async_computation.2 | async-start | bytes 1769472 | tf_op jit(solution)/shard_map/psum | solution.py:155
  138.2 6.9 %collective-permute-start.11 = (bf16[128,3,1,128]{0,3,2,1:T(8,128)(2,1)S(1)}, bf16[128,3,1,128]{0,3,2,1:T(8,128)(2,1)S(1)}, u32[]{:S(2)}, u32[]{:S(2)}) collective-permute-start(bf16[128,3,1,128]{0,3,2,1:T(8,128)(2,1)S(1)} %pad_maximum_fusion.17), channel_id=1, source_target_pairs={{1,0},{3,2},{5,4},{7,6},{9,8},{11,10},{13,12},{15,14},{17,16},{19,... | collective-permute-start | bytes 294920 | tf_op jit(solution)/shard_map/ppermute | solution.py:17
  139.5 6.8 %collective-permute-start.10 = (bf16[128,3,1,128]{0,3,2,1:T(8,128)(2,1)S(1)}, bf16[128,3,1,128]{0,3,2,1:T(8,128)(2,1)S(1)}, u32[]{:S(2)}, u32[]{:S(2)}) collective-permute-start(bf16[128,3,1,128]{0,3,2,1:T(8,128)(2,1)S(1)} %pad_maximum_fusion.17), channel_id=1, source_target_pairs={{0,1},{2,3},{4,5},{6,7},{8,9},{10,11},{12,13},{14,15},{16,17},{18,... | collective-permute-start | bytes 294920 | tf_op jit(solution)/shard_map/ppermute | solution.py:15
  157.9 6.4 %collective-permute-start.13 = (bf16[64,1,2,256]{3,2,1,0:T(2,128)(2,1)S(1)}, bf16[64,1,2,256]{3,2,1,0:T(2,128)(2,1)S(1)}, u32[]{:S(2)}, u32[]{:S(2)}) collective-permute-start(bf16[64,1,2,256]{3,2,1,0:T(2,128)(2,1)S(1)} %get-tuple-element.269), channel_id=1, source_target_pairs={{2,0},{4,2},{6,4},{8,6},{10,8},{12,10},{14,12},{16,14},{18,16},{20... | collective-permute-start | bytes 196616 | tf_op jit(solution)/shard_map/ppermute | solution.py:17
  159.2 5.1 %collective-permute-start.12 = (bf16[64,1,2,256]{3,2,1,0:T(2,128)(2,1)S(1)}, bf16[64,1,2,256]{3,2,1,0:T(2,128)(2,1)S(1)}, u32[]{:S(2)}, u32[]{:S(2)}) collective-permute-start(bf16[64,1,2,256]{3,2,1,0:T(2,128)(2,1)S(1)} %get-tuple-element.270), channel_id=1, source_target_pairs={{0,2},{2,4},{4,6},{6,8},{8,10},{10,12},{12,14},{14,16},{16,18},{18... | collective-permute-start | bytes 196616 | tf_op jit(solution)/shard_map/ppermute | solution.py:15
  164.2 236.0 %all-reduce.12.cloned.1.call-start = ((), (), s32[]{:S(2)}) async-start(), calls=%async_computation.4 | async-start | bytes 3538944 | tf_op jit(solution)/shard_map/psum | solution.py:134
  165.2 9.6 %collective-permute-start.14 = (bf16[64,4,1,256]{3,2,1,0:T(2,128)(2,1)S(1)}, bf16[64,4,1,256]{3,2,1,0:T(2,128)(2,1)S(1)}, u32[]{:S(2)}, u32[]{:S(2)}) collective-permute-start(bf16[64,4,1,256]{3,2,1,0:T(2,128)(2,1)S(1)} %get-tuple-element.259), channel_id=1, source_target_pairs={{0,1},{2,3},{4,5},{6,7},{8,9},{10,11},{12,13},{14,15},{16,17},{18,... | collective-permute-start | bytes 393224 | tf_op jit(solution)/shard_map/ppermute | solution.py:15
  169.2 10.3 %collective-permute-start.15 = (bf16[64,4,1,256]{3,2,1,0:T(2,128)(2,1)S(1)}, bf16[64,4,1,256]{3,2,1,0:T(2,128)(2,1)S(1)}, u32[]{:S(2)}, u32[]{:S(2)}) collective-permute-start(bf16[64,4,1,256]{3,2,1,0:T(2,128)(2,1)S(1)} %get-tuple-element.260), channel_id=1, source_target_pairs={{1,0},{3,2},{5,4},{7,6},{9,8},{11,10},{13,12},{15,14},{17,16},{19,... | collective-permute-start | bytes 393224 | tf_op jit(solution)/shard_map/ppermute | solution.py:17
  171.3 267.6 %all-reduce.10.cloned.1.call-start = ((), (), s32[]{:S(2)}) async-start(), calls=%async_computation.3 | async-start | bytes 1769472 | tf_op jit(solution)/shard_map/psum | solution.py:155
  191.8 71.4 %copy-start.72 = (bf16[3,64,64]{2,1,0:T(8,128)(2,1)S(1)}, bf16[3,64,64]{2,1,0:T(8,128)(2,1)}, u32[]{:S(2)}) copy-start(bf16[3,64,64]{2,1,0:T(8,128)(2,1)} %rev.97) | copy-start | bytes 73732
  192.1 71.5 %copy-start.71 = (bf16[3,64,64]{2,1,0:T(8,128)(2,1)S(1)}, bf16[3,64,64]{2,1,0:T(8,128)(2,1)}, u32[]{:S(2)}) copy-start(bf16[3,64,64]{2,1,0:T(8,128)(2,1)} %rev.98) | copy-start | bytes 73732
  (59 other events, 181.9 us)
Sparse Core Ops, SparseCore 0:
  164.4 98.6 all-reduce.7
  268.5 131.7 all-reduce.11
  402.6 36.2 all-reduce.9
